TPU v7x, 512 devices: a whole 4x4x16 slice. The times are simulated.
512 devices in a mesh: wide: 64 (over y, z_lo, core), narrow: 8 (over x, z_hi).
Axes of the slice: x: 4, y: 4, z: 16 (z_hi: 2, z_lo: 8; z = z_hi * 8 + z_lo), core: 2. Of those that a mesh axis runs over, the one named last changes fastest.
Arguments:
- lifted_field: bfloat16 [64, 32, 64, 128], P('wide', None, 'narrow'), may hold values from -6 to 6
- spectral_weight: float32 [256, 16, 2, 32, 32], P('wide', 'narrow'), may hold values from -0.75 to 0.75
- mix_weight: bfloat16 [32, 32], replicated, may hold values from -1 to 1
- mix_bias: float32 [32], replicated, may hold values from -3 to 3
- head_weight: bfloat16 [32, 128], replicated, may hold values from -1 to 1
- head_bias: float32 [128], replicated, may hold values from -3 to 3
- out_weight: bfloat16 [128], replicated, may hold values from -0.5 to 0.5
- cotangent: float32 [64, 64, 128], P('wide', 'narrow'), may hold values from -6 to 6
Outputs:
- prediction: float32 [64, 64, 128], P('wide', 'narrow')
- grad_field: bfloat16 [64, 32, 64, 128], P('wide', None, 'narrow')
- grad_spectral: float32 [256, 16, 2, 32, 32], P('wide', 'narrow')
- grad_mix: float32 [32, 32], replicated
- grad_head: float32 [32, 128], replicated
All inputs are finite; a program needn't handle non-finite values.
Results may differ from a plain program's by a relative error of at most 0.018.
Values may be sent and summed in bfloat16 or wider, within the bound.
A program may use at most 64 MiB of HBM per device.

v0:
```python
import math

import jax
import jax.numpy as jnp
from jax import lax
from jax.sharding import PartitionSpec as P

MX = 16
MY = 16
MZ = 16


HIGHEST_PRECISION = lax.Precision.HIGHEST


def signed_freq(indices, kept_count):
    return jnp.where(indices < kept_count // 2, indices, indices - kept_count)


def phases(positions, frequency, length):
    turned = jnp.mod(positions[:, None] * frequency[None, :], length)
    return turned.astype(jnp.float32) * (2.0 * math.pi / length)


def real_forward(positions, length, kept_count, doubled):
    indices = jnp.arange(kept_count, dtype=jnp.int32)
    angles = phases(positions, indices, length)
    if doubled:
        scaling = 1.0 + (indices > 0).astype(jnp.float32)
    else:
        scaling = jnp.ones((kept_count,), jnp.float32)
    scaling = scaling * (1.0 / math.sqrt(length))
    return jnp.stack([jnp.cos(angles) * scaling, -jnp.sin(angles) * scaling], axis=1)


def real_inverse(positions, length, kept_count, doubled):
    return jnp.transpose(real_forward(positions, length, kept_count, doubled), (2, 1, 0))


def complex_forward(positions, frequency, length):
    angles = phases(positions, frequency, length)
    cosine = jnp.cos(angles) * (1.0 / math.sqrt(length))
    sine = jnp.sin(angles) * (1.0 / math.sqrt(length))
    return jnp.stack([jnp.stack([cosine, sine]), jnp.stack([-sine, cosine])])


def complex_inverse(positions, frequency, length):
    angles = phases(positions, frequency, length)
    cosine = jnp.transpose(jnp.cos(angles)) * (1.0 / math.sqrt(length))
    sine = jnp.transpose(jnp.sin(angles)) * (1.0 / math.sqrt(length))
    return jnp.stack([jnp.stack([cosine, -sine]), jnp.stack([sine, cosine])])


def activation(values):
    return jax.nn.gelu(values, approximate=False)


def activation_slope(values):
    cumulative = 0.5 * (1.0 + lax.erf(values * (1.0 / math.sqrt(2.0))))
    return cumulative + values * jnp.exp(-0.5 * values * values) * (1.0 / math.sqrt(2.0 * math.pi))


def mode_forward(spectrum, weights):
    real_part = spectrum[:, :, 0]
    imag_part = spectrum[:, :, 1]
    real_weight = weights[:, :, 0]
    imag_weight = weights[:, :, 1]

    def combine(spectrum_part, weight_part):
        return jnp.einsum("mki,mkio->mko", spectrum_part, weight_part, precision=HIGHEST_PRECISION)

    out_real = combine(real_part, real_weight) - combine(imag_part, imag_weight)
    out_imag = combine(imag_part, real_weight) + combine(real_part, imag_weight)
    return jnp.stack([out_real, out_imag], axis=2)


def mode_backward(spectrum, weights, gradient):
    real_part = spectrum[:, :, 0]
    imag_part = spectrum[:, :, 1]
    real_weight = weights[:, :, 0]
    imag_weight = weights[:, :, 1]
    real_grad = gradient[:, :, 0]
    imag_grad = gradient[:, :, 1]

    def pulled(weight_part, grad_part):
        return jnp.einsum("mkio,mko->mki", weight_part, grad_part, precision=HIGHEST_PRECISION)

    def product(spectrum_part, grad_part):
        return jnp.einsum("mki,mko->mkio", spectrum_part, grad_part, precision=HIGHEST_PRECISION)

    back_real = pulled(real_weight, real_grad) + pulled(imag_weight, imag_grad)
    back_imag = pulled(real_weight, imag_grad) - pulled(imag_weight, real_grad)
    weight_real = product(real_part, real_grad) + product(imag_part, imag_grad)
    weight_imag = product(real_part, imag_grad) - product(imag_part, real_grad)
    return (
        jnp.stack([back_real, back_imag], axis=2),
        jnp.stack([weight_real, weight_imag], axis=2),
    )


def body(
    lifted_field,
    spectral_weight,
    mix_weight,
    mix_bias,
    head_weight,
    head_bias,
    out_weight,
    cotangent,
):
    wide_count = lax.axis_size("wide")
    narrow_count = lax.axis_size("narrow")
    rows_x, channels, rows_y, z_count = lifted_field.shape
    total_x = rows_x * wide_count
    total_y = rows_y * narrow_count
    wide_index = lax.axis_index("wide")
    x_cells = wide_index * rows_x + jnp.arange(rows_x, dtype=jnp.int32)
    y_every = jnp.arange(total_y, dtype=jnp.int32)
    z_cells = jnp.arange(z_count, dtype=jnp.int32)
    y_freq = signed_freq(jnp.arange(MY, dtype=jnp.int32), MY)
    column_ids = jnp.arange(MY, dtype=jnp.int32)
    mode_rows = MX * MY // wide_count

    def mode_tables(row_count):
        mode_ids = jnp.arange(row_count, dtype=jnp.int32)
        selector = (mode_ids[:, None] % MY == column_ids[None, :]).astype(jnp.float32)
        return (signed_freq(mode_ids // MY, MX), selector)

    def analysis(values, doubled):
        z_table = real_forward(z_cells, z_count, MZ, doubled).astype(jnp.bfloat16)
        spectra = jnp.einsum(
            "xcyz,zrk->krcxy", values, z_table, preferred_element_type=jnp.float32
        ).astype(jnp.bfloat16)
        regrouped = lax.all_to_all(spectra, "narrow", split_axis=0, concat_axis=4, tiled=True)
        y_table = complex_forward(y_every, y_freq, total_y).astype(jnp.bfloat16)
        planes = jnp.einsum(
            "krcxn,srnj->kscxj", regrouped, y_table, preferred_element_type=jnp.float32
        )
        frequency, selector = mode_tables(mode_rows * lax.axis_size("wide"))
        x_table = complex_forward(x_cells, frequency, total_x)
        chosen = jnp.einsum("kscxj,mj->mkscx", planes, selector, precision=HIGHEST_PRECISION)
        return lax.psum_scatter(
            jnp.einsum("mkscx,tsxm->mktc", chosen, x_table, precision=HIGHEST_PRECISION),
            "wide",
            scatter_dimension=0,
            tiled=True,
        )

    def synthesis(spectrum, doubled):
        shard_piece = lax.all_gather(spectrum, "wide", axis=0, tiled=True)
        frequency, selector = mode_tables(shard_piece.shape[0])
        x_table = complex_inverse(x_cells, frequency, total_x).astype(jnp.bfloat16)
        turned = jnp.einsum(
            "mkrc,srmx->mkscx", shard_piece, x_table, preferred_element_type=jnp.float32
        )
        planes = jnp.einsum(
            "mkscx,mj->kscxj", turned, selector, precision=HIGHEST_PRECISION
        ).astype(jnp.bfloat16)
        y_table = complex_inverse(y_every, y_freq, total_y).astype(jnp.bfloat16)
        line_data = jnp.einsum(
            "krcxj,srjn->kscxn", planes, y_table, preferred_element_type=jnp.float32
        ).astype(jnp.bfloat16)
        line_data = lax.all_to_all(line_data, "narrow", split_axis=4, concat_axis=0, tiled=True)
        z_table = real_inverse(z_cells, z_count, MZ, doubled).astype(jnp.bfloat16)
        return jnp.einsum("krcxy,krz->xcyz", line_data, z_table, preferred_element_type=jnp.float32)

    spectrum = analysis(lifted_field, False)
    mode = mode_forward(spectrum, spectral_weight).astype(jnp.bfloat16)
    mixed = jnp.einsum(
        "xcyz,cd->xdyz", lifted_field, mix_weight, preferred_element_type=jnp.float32
    )
    pre_act = synthesis(mode, True) + mixed + mix_bias[None, :, None, None]

    def head_row(row_items):
        pre_row, target_row = row_items
        hidden = activation(pre_row).astype(jnp.bfloat16)
        head_pre = (
            jnp.einsum("cyz,cj->jyz", hidden, head_weight, preferred_element_type=jnp.float32)
            + head_bias[:, None, None]
        )
        active = activation(head_pre).astype(jnp.bfloat16)
        predicted = jnp.einsum("jyz,j->yz", active, out_weight, preferred_element_type=jnp.float32)
        head_slope = (
            target_row[None]
            * out_weight.astype(jnp.float32)[:, None, None]
            * activation_slope(head_pre)
        ).astype(jnp.bfloat16)
        returned = jnp.einsum(
            "jyz,cj->cyz", head_slope, head_weight, preferred_element_type=jnp.float32
        )
        grad_row = (returned * activation_slope(pre_row)).astype(jnp.bfloat16)
        head_grad = jnp.einsum(
            "cyz,jyz->cj", hidden, head_slope, preferred_element_type=jnp.float32
        )
        return (predicted, grad_row, head_grad)

    prediction, grad_pre, head_parts = lax.map(head_row, (pre_act, cotangent))
    adjoint = analysis(grad_pre, True)
    back_modes, grad_spectral = mode_backward(spectrum, spectral_weight, adjoint)
    field_back = synthesis(back_modes.astype(jnp.bfloat16), False) + jnp.einsum(
        "xdyz,cd->xcyz", grad_pre, mix_weight, preferred_element_type=jnp.float32
    )
    grad_field = field_back.astype(jnp.bfloat16)
    mix_terms = jnp.einsum(
        "xcyz,xdyz->cd", lifted_field, grad_pre, preferred_element_type=jnp.float32
    )
    grad_mix, grad_head = lax.psum((mix_terms, jnp.sum(head_parts, axis=0)), ("wide", "narrow"))
    return (prediction, grad_field, grad_spectral, grad_mix, grad_head)


def solution(mesh):
    return jax.shard_map(
        body,
        mesh=mesh,
        in_specs=(
            P("wide", None, "narrow", None),
            P("wide", "narrow", None, None, None),
            P(),
            P(),
            P(),
            P(),
            P(),
            P("wide", "narrow", None),
        ),
        out_specs=(
            P("wide", "narrow", None),
            P("wide", None, "narrow", None),
            P("wide", "narrow", None, None, None),
            P(),
            P(),
        ),
        check_vma=False,
    )
```

profile of v0, /device:TPU:1, one launch (start us, length us, event | category | flops | bytes accessed | tf_op | source)
XLA Modules:
  0.0 2005.2 jit_solution(6915720392078223617)
XLA Ops:
  7.2 1.0 fusion.8
  8.3 0.7 reshape.817
  9.1 18.1 all-to-all-start
  28.1 12.8 all-to-all-done
  41.8 2.8 convolution_bitcast_fusion.3
  44.9 1.3 dynamic-slice
  46.8 816.1 %all-reduce.6.cloned.1.call-done = f32[256,2,2,32]{3,2,1,0:T(2,128)} async-done(((f32[256,2,2,32]{3,2,1,0:T(2,128)}), f32[256,2,2,32]{3,2,1,0:T(2,128)}) %all-reduce.6.cloned.1.call-update) | async-done | bytes 131088
  863.0 0.8 constant_dynamic-slice_fusion.1
  864.7 123.1 %all_gather.6 = bf16[256,2,2,32]{3,2,1,0:T(2,128)(2,1)S(1)} all-gather(bf16[4,2,2,32]{3,2,1,0:T(2,128)(2,1)S(1)} %copy.89), channel_id=1, replica_groups=mesh['wide'=64,'narrow'=8] {'wide'}, dimensions={0}, use_global_device_ids=true | all-gather | bytes 66560 | tf_op jit(solution)/shard_map/all_gather | solution.py:150
  988.9 0.7 reshape.819
  989.6 6.9 all-to-all-start.1
  997.2 13.1 all-to-all-done.1
  1012.8 1.9 fusion.36
  1015.1 0.7 reshape.821
  1015.8 3.3 all-to-all-start.2
  1019.4 13.5 all-to-all-done.2
  1033.8 2.8 convolution_bitcast_fusion.1
  1036.7 100.7 %all-reduce.2 = (f32[32,32]{0,1:T(8,128)S(1)}, f32[32,128]{1,0:T(8,128)}) all-reduce(f32[32,32]{0,1:T(8,128)S(1)} %convolution_bitcast_fusion.14, f32[32,128]{1,0:T(8,128)S(1)} %convolution_bitcast_fusion.13), channel_id=1, replica_groups=mesh['wide'=64,'narrow'=8] {'wide','narrow'}, use_global_device_ids=true, to_apply=%region_2.3 | all-reduce | flops 5120 | bytes 40960 | tf_op jit(solution)/shard_map/psum | solution.py:207
  1138.2 711.6 %all-reduce.8.cloned.1.call-done = f32[256,2,2,32]{3,2,1,0:T(2,128)} async-done(((f32[256,2,2,32]{3,2,1,0:T(2,128)}), f32[256,2,2,32]{3,2,1,0:T(2,128)}) %all-reduce.8.cloned.1.call-update) | async-done | bytes 131088
  1849.8 0.8 constant_dynamic-slice_fusion
  1851.9 123.1 %all_gather.7 = bf16[256,2,2,32]{3,2,1,0:T(2,128)(2,1)S(1)} all-gather(bf16[4,2,2,32]{3,2,1,0:T(2,128)(2,1)S(1)} %copy.103), channel_id=1, replica_groups=mesh['wide'=64,'narrow'=8] {'wide'}, dimensions={0}, use_global_device_ids=true | all-gather | bytes 66560 | tf_op jit(solution)/shard_map/all_gather | solution.py:150
  1976.7 6.8 all-to-all-start.3
  1983.7 0.7 pad_maximum_fusion
  1984.4 12.9 all-to-all-done.3
  (93 shorter events, 13.7 us)
Async XLA Ops:
  7.2 1004.5 %copy-start = (bf16[32,128]{1,0:T(8,128)(2,1)S(1)}, bf16[32,128]{1,0:T(8,128)(2,1)}, u32[]{:S(2)}) copy-start(bf16[32,128]{1,0:T(8,128)(2,1)} %param.12) | copy-start | bytes 24580
  9.1 31.9 %all-to-all-start = ((bf16[8,2,512]{2,1,0:T(2,128)(2,1)}), bf16[8,2,512]{2,1,0:T(2,128)(2,1)S(1)}, u32[]{:S(2)}, u32[]{:S(2)}) async-start(bf16[8,2,512]{2,1,0:T(2,128)(2,1)} %reshape.817), calls=%async_computation | async-start | bytes 32768 | tf_op jit(solution)/shard_map/all_to_all | solution.py:134
  27.2 835.8 %all-reduce.6.cloned.1.call-start = ((), (), s32[]{:S(2)}) async-start(), calls=%async_computation.4 | async-start | bytes 1048576
  44.6 819.1 %copy-start.1 = (f32[4,2,2,32,32]{4,3,2,1,0:T(8,128)S(1)}, f32[4,2,2,32,32]{4,3,2,1,0:T(8,128)}, u32[]{:S(2)}) copy-start(f32[4,2,2,32,32]{4,3,2,1,0:T(8,128)} %param.9) | copy-start | bytes 196612
  988.9 7.7 copy-start.2
  989.6 7.0 copy-start.3
  989.6 20.7 %all-to-all-start.1 = ((bf16[8,2,512]{2,1,0:T(2,128)(2,1)}), bf16[8,2,512]{2,1,0:T(2,128)(2,1)S(1)}, u32[]{:S(2)}, u32[]{:S(2)}) async-start(bf16[8,2,512]{2,1,0:T(2,128)(2,1)} %reshape.819), calls=%async_computation.1 | async-start | bytes 32768 | tf_op jit(solution)/shard_map/all_to_all | solution.py:163
  996.6 0.7 copy-start.7
  1010.5 0.7 copy-start.5
  1011.2 0.7 copy-start.4
  1011.7 0.7 copy-start.6
  1015.8 17.0 all-to-all-start.2
  1019.2 830.6 %all-reduce.8.cloned.1.call-start = ((), (), s32[]{:S(2)}) async-start(), calls=%async_computation.5 | async-start | bytes 1048576
  1976.7 20.6 %all-to-all-start.3 = ((bf16[8,2,512]{2,1,0:T(2,128)(2,1)}), bf16[8,2,512]{2,1,0:T(2,128)(2,1)S(1)}, u32[]{:S(2)}, u32[]{:S(2)}) async-start(bf16[8,2,512]{2,1,0:T(2,128)(2,1)} %reshape.823), calls=%async_computation.3 | async-start | bytes 32768 | tf_op jit(solution)/shard_map/all_to_all | solution.py:163
Sparse Core Ops, SparseCore 0:
  44.8 818.1 all-reduce.5
  1036.7 813.0 all-reduce.7
where the time goes:
time: 2010 us
  waiting for transfers between devices  1580 us (79%)
  blocking collectives  347 us (17%)
  starting transfers between devices  35.3 us (2%)
    unnamed x4, waiting for transfers between devices  1530 us
    all_gather x2, blocking collectives, synthesis(): shard_piece = lax.all_gather(spectrum, 'wide', axis=0, tiled=True)  246 us
    psum x1, blocking collectives, body(): lax.psum((mix_terms, jnp.sum(head_parts, axis=0)), ('wide', 'narrow'))  101 us
  transfers between devices with their start and end apart: 6, of which 6 were waited for; matrix products, arithmetic and copies ran while one was open for 0% of the time, Pallas kernels for 0%

commit v1 on v0

v1 whole, which is shorter than its diff:
```python
import functools
import math

import jax
import jax.numpy as jnp
import ml_dtypes
import numpy as np
from jax import lax
from jax.experimental import pallas as pl
from jax.experimental.pallas import tpu as pltpu
from jax.sharding import PartitionSpec as P

MESH = pl.DeviceIdType.MESH
BF = jnp.bfloat16
F32 = jnp.float32
NX, NY, NZ, C, HID = 64, 64, 128, 32, 128
CROSS = [(dx, dy, dc) for dx in range(4) for dy in range(4) for dc in range(2) if dx or dy or dc]
CROSS.sort(key=lambda t: (-(min(t[0], 4 - t[0]) + min(t[1], 4 - t[1])), t))
RING = sorted(range(1, 16), key=lambda d: (-min(d, 16 - d), d))


def angle(position, frequency, length):
    return 2.0 * math.pi * ((position * frequency) % length) / length


def narrow_type(table):
    return np.asarray(table, np.float32).astype(ml_dtypes.bfloat16)


@functools.lru_cache(None)
def z_tables():
    forward = np.zeros((2, 2, 4, 2, 4, NZ))
    inverse = np.zeros((2, 2, 4, 2, 4, NZ))
    z = np.arange(NZ)
    for flag in range(2):
        for k in range(16):
            scale = (2.0 if flag and k else 1.0) / math.sqrt(NZ)
            real, imag = scale * np.cos(angle(z, k, NZ)), -scale * np.sin(angle(z, k, NZ))
            x, kk = k // 4, k % 4
            forward[flag, 0, x, 0, kk], forward[flag, 0, x, 1, kk] = real, imag
            forward[flag, 1, x, 0, kk], forward[flag, 1, x, 1, kk] = imag, -real
            inverse[flag, 0, x, 0, kk], inverse[flag, 0, x, 1, kk] = real, imag
            inverse[flag, 1, x, 0, kk], inverse[flag, 1, x, 1, kk] = imag, -real
    return narrow_type(forward.reshape(2, 64, NZ)), narrow_type(inverse.reshape(2, 64, NZ))


def frequency(i):
    return i if i < 8 else i - 16


@functools.lru_cache(None)
def y_tables():
    out = np.zeros((8, 2, 8, 16, C), np.float32)
    for n in range(8):
        for y in range(8):
            for place in range(16):
                core, par, low = place // 8, (place // 4) % 2, place % 4
                theta = angle(8 * n + y, frequency((2 * par + core) * 4 + low), NY)
                out[n, 0, y, place] = math.cos(theta) / 8.0
                out[n, 1, y, place] = math.sin(theta) / 8.0
    return out.reshape(8, 16, 512)


@functools.lru_cache(None)
def x_tables():
    forward = np.zeros((4, 8, 16, 2, 2, 4, 2, 2, 2, 4), np.float32)
    inverse = np.zeros((4, 8, 16, 2, 2, 4, 2, 2, 2, 4), np.float32)
    for y in range(4):
        for zl in range(8):
            for i4 in range(4):
                for y2 in range(4):
                    for c2 in range(2):
                        theta = angle(16 * y2 + 2 * zl + c2, frequency(4 * y + i4), NX)
                        co, si = math.cos(theta) / 8.0, math.sin(theta) / 8.0
                        for par in range(2):
                            for zh in range(2):
                                for k2 in range(2):
                                    z2, kk = zh * 8 + 2 * i4 + par, 2 * zh + k2
                                    for s, t, value in ((0, 0, co), (0, 1, si), (1, 0, -si), (1, 1, co)):
                                        forward[y, zl, z2, s, k2, y2, c2, par, t, kk] = value
                                    for s, t, value in ((0, 0, co), (0, 1, -si), (1, 0, si), (1, 1, co)):
                                        inverse[y, zl, z2, t, k2, y2, c2, par, s, kk] = value
    return narrow_type(forward.reshape(32, 64, 128)), narrow_type(inverse.reshape(32, 64, 128))


def dot(a, b, dims):
    return lax.dot_general(a, b, ((dims[:1], dims[1:]), ((), ())), preferred_element_type=F32)


def gelu_parts(v):
    cumulative = 0.5 * (1.0 + lax.erf(v * (1.0 / math.sqrt(2.0))))
    bell = jnp.exp(-0.5 * v * v) * (1.0 / math.sqrt(2.0 * math.pi))
    return v * cumulative, cumulative + v * bell


def column(row, rows):
    return jnp.transpose(jnp.broadcast_to(row, (128, rows)))


def kernel(
    v_hbm, w_hbm, mix_hbm, bias_hbm, head_hbm, hb_hbm, ow_hbm, cot_hbm, ez_hbm, ei_hbm, r_hbm, t1_hbm, t2_hbm,
    pred_out, field_out, spec_out, mixg_out, headg_out,
    v_in, w_in, mix_in, bias_in, head_in, hb_in, ow_in, cot_in, ez_in, ei_in, r_rows, t1_in, t2_in, r_in,
    vf, vy, wst, wcat, mixed, hidden, gp, slope, gpre, fin, lhs, zrow, srow, arow,
    pred_s, field_s, spec_s, mixg_s, headg_s,
    asend, arecv, bsend, brecv, csend, crecv, dsend, drecv,
    g1send, g1recv, g2send, g2recv, g3recv,
    in_sem, out_sem, send_sem, recv_sem,
):
    w = lax.axis_index("wide")
    n = lax.axis_index("narrow")
    y, zl, c = w // 16, lax.rem(w // 2, 8), lax.rem(w, 2)
    x, zh = n // 2, lax.rem(n, 2)
    q = x * 8 + y * 2 + c
    z = zh * 8 + zl

    cross = []
    for dx, dy, dc in CROSS:
        x2, y2, c2 = lax.rem(x + dx, 4), lax.rem(y + dy, 4), lax.rem(c + dc, 2)
        cross.append((x2, y2, c2, (y2 * 16 + zl * 2 + c2, x2 * 2 + zh)))
    ring = []
    for d in RING:
        z2 = lax.rem(z + d, 16)
        ring.append((z2, (y * 16 + lax.rem(z2, 8) * 2 + c, x * 2 + z2 // 8)))

    barrier = pltpu.get_barrier_semaphore()
    for *_, where in ring:
        pl.semaphore_signal(barrier, inc=1, device_id=where, device_id_type=MESH)
    for *_, where in cross:
        pl.semaphore_signal(barrier, inc=1, device_id=where, device_id_type=MESH)

    variant = y * 8 + zl
    loads = [
        (v_hbm, v_in), (ez_hbm, ez_in), (r_hbm.at[n], r_rows), (t1_hbm.at[variant], t1_in), (w_hbm, w_in),
        (mix_hbm, mix_in), (bias_hbm, bias_in), (head_hbm, head_in), (hb_hbm, hb_in), (ow_hbm, ow_in),
        (cot_hbm, cot_in), (ei_hbm, ei_in), (t2_hbm.at[variant], t2_in),
    ]
    loads = [pltpu.make_async_copy(a, b, in_sem.at[i]) for i, (a, b) in enumerate(loads)]
    for load in loads:
        load.start()

    def send(source, target, where, stage):
        pltpu.make_async_remote_copy(
            src_ref=source, dst_ref=target, send_sem=send_sem.at[stage], recv_sem=recv_sem.at[stage],
            device_id=where, device_id_type=MESH,
        ).start()

    def arrived(buffer, count, stage):
        part = buffer.at[pl.ds(0, count)]
        pltpu.make_async_copy(part, part, recv_sem.at[stage]).wait()

    def sent(buffer, count, stage):
        part = buffer.at[pl.ds(0, count)]
        pltpu.make_async_copy(part, part, send_sem.at[stage]).wait()

    def local_analysis(values, flag, turn):
        spectra = dot(ez_in[flag], values, (1, 1)).astype(BF)
        planes = dot(spectra[:32], r_in[:256], (1, 0)) + dot(spectra[32:], r_in[256:], (1, 0))
        for x2 in range(4):
            for c2 in range(2):
                first = planes[8 * x2 : 8 * x2 + 8, 256 * c2 : 256 * c2 + 128]
                second = planes[8 * x2 : 8 * x2 + 8, 256 * c2 + 128 : 256 * c2 + 256]
                asend[turn, x2 * 2 + c2] = jnp.concatenate([first, second], axis=0).astype(BF)
        arecv[turn, q] = asend[turn, x * 2 + c]

    def analysis_send(turn):
        for x2, y2, c2, where in cross:
            send(asend.at[turn, x2 * 2 + c2], arecv.at[turn, q], where, 4 * turn)

    def analysis_middle(turn):
        arrived(arecv.at[turn], 31, 4 * turn)
        table = t1_in[...]
        table = jnp.concatenate([table] * 4, axis=1)
        partial = dot(table, arecv[turn].reshape(512, 128), (1, 0))
        for z2 in range(16):
            bsend[turn, z2] = partial[4 * z2 : 4 * z2 + 4]
        brecv[turn, z] = bsend[turn, z]
        for z2, where in ring:
            send(bsend.at[turn, z2], brecv.at[turn, z], where, 4 * turn + 1)

    def analysis_end(turn):
        arrived(brecv.at[turn], 15, 4 * turn + 1)
        total = brecv[turn, 0]
        for z2 in range(1, 16):
            total = total + brecv[turn, z2]
        return total

    def paired(spectrum, low_sign, high_sign):
        srow[0:2] = low_sign * spectrum[2:4]
        srow[2:4] = high_sign * spectrum[0:2]
        turned = srow[0:4]
        row = lax.broadcasted_iota(jnp.int32, (4, 128), 0)
        even = lax.rem(row, 2) == 0
        parts = [
            jnp.where(even, spectrum, 0.0), jnp.where(even, turned, 0.0),
            jnp.where(even, 0.0, spectrum), jnp.where(even, 0.0, turned),
        ]
        return jnp.concatenate(parts, axis=1).astype(BF)

    def synthesis_start(modes, turn):
        csend[turn] = modes
        crecv[turn, z] = modes
        for z2, where in ring:
            send(csend.at[turn], crecv.at[turn, z], where, 4 * turn + 2)

    def synthesis_middle(turn):
        arrived(crecv.at[turn], 15, 4 * turn + 2)
        for z2 in range(16):
            zrow[4 * z2 : 4 * z2 + 4] = crecv[turn, z2]
        planes = dot(t2_in[...], zrow[...].astype(BF), (0, 0)).astype(BF)
        for piece in range(8):
            dsend[turn, piece] = planes[16 * piece : 16 * piece + 16]
        drecv[turn, q] = dsend[turn, y * 2 + c]
        for x2, y2, c2, where in cross:
            send(dsend.at[turn, y2 * 2 + c2], drecv.at[turn, q], where, 4 * turn + 3)

    def synthesis_end(flag, turn):
        arrived(drecv.at[turn], 31, 4 * turn + 3)
        for x2 in range(4):
            for c2 in range(2):
                block = drecv[turn, x2 * 8 + c2].astype(F32)
                for y2 in range(1, 4):
                    block = block + drecv[turn, x2 * 8 + y2 * 2 + c2].astype(F32)
                lhs[8 * x2 : 8 * x2 + 8, 256 * c2 : 256 * c2 + 128] = block[:8]
                lhs[8 * x2 : 8 * x2 + 8, 256 * c2 + 128 : 256 * c2 + 256] = block[8:]
        lines = dot(lhs[...].astype(BF), r_in[...], (1, 1)).astype(BF)
        stacked = jnp.concatenate([lines[:, :256], lines[:, 256:]], axis=0)
        return dot(stacked, ei_in[flag], (0, 0))

    for i in (0, 1, 2):
        loads[i].wait()
    keep = lax.rem(lax.broadcasted_iota(jnp.int32, (32, 512), 1), 32) == lax.broadcasted_iota(jnp.int32, (32, 512), 0)
    for row in range(16):
        spread = jnp.broadcast_to(r_rows[row : row + 1], (32, 512))
        r_in[32 * row : 32 * row + 32] = jnp.where(keep, spread, 0.0).astype(BF)
    vf[...] = v_in[...].astype(F32)
    for row in range(8):
        vy[32 * row : 32 * row + 32] = vf[pl.ds(row, 32, stride=8), :].astype(BF)
    local_analysis(vy[...], 0, 0)

    for load in loads[3:]:
        load.wait()
    for k2 in range(2):
        for r in range(2):
            for j4 in range(4):
                block = w_in[j4, k2, r].astype(BF)
                zero = jnp.zeros((32, 32), BF)
                wide = jnp.concatenate([zero] * j4 + [block] + [zero] * (3 - j4), axis=1)
                base = 128 * (2 * k2 + r)
                wst[base + 32 * j4 : base + 32 * j4 + 32] = wide
                wcat[32 * j4 : 32 * j4 + 32, base : base + 128] = wide
    bias_col = column(bias_in[...], 32)
    for row in range(8):
        mixed[32 * row : 32 * row + 32] = dot(mix_in[...], vy[32 * row : 32 * row + 32], (0, 0)) + bias_col
    head_col = column(hb_in[...], 128)
    out_col = column(ow_in[...].astype(F32), 128)

    pl.semaphore_wait(barrier, len(CROSS) + len(RING))
    analysis_send(0)
    analysis_middle(0)
    spectrum = analysis_end(0)
    modes = dot(paired(spectrum, -1.0, 1.0), wst[...], (1, 0))
    synthesis_start(modes, 0)
    synthesis_middle(0)
    pre = synthesis_end(1, 0) + mixed[...]

    value, rate = gelu_parts(pre)
    hidden[...] = value.astype(BF)
    gp[...] = rate
    for row in range(8):
        head_pre = dot(head_in[...], hidden[32 * row : 32 * row + 32], (0, 0)) + head_col
        value, rate = gelu_parts(head_pre)
        pred_s[row : row + 1] = dot(ow_in[...], value.astype(BF), (1, 0))
        slope[128 * row : 128 * row + 128] = (cot_in[row : row + 1] * out_col * rate).astype(BF)
        back = dot(head_in[...], slope[128 * row : 128 * row + 128], (1, 0))
        gpre[32 * row : 32 * row + 32] = (back * gp[32 * row : 32 * row + 32]).astype(BF)
    stores = [pltpu.make_async_copy(pred_s, pred_out, out_sem.at[0])]
    stores[0].start()
    local_analysis(gpre[...], 1, 1)
    analysis_send(1)

    head_grad = jnp.zeros((32, 128), F32)
    mix_grad = jnp.zeros((32, 32), F32)
    for row in range(8):
        head_grad = head_grad + dot(hidden[32 * row : 32 * row + 32], slope[128 * row : 128 * row + 128], (1, 1))
        mix_grad = mix_grad + dot(vy[32 * row : 32 * row + 32], gpre[32 * row : 32 * row + 32], (1, 1))
    folded = jnp.concatenate([mix_grad[8 * i : 8 * i + 8] for i in range(4)], axis=1)
    for i in range(16):
        g1send[i] = head_grad[2 * i : 2 * i + 2]
    for i in range(4):
        g1send[16 + i] = folded[2 * i : 2 * i + 2]
    for i in range(20, 32):
        g1send[i] = jnp.zeros((2, 128), F32)
    g1recv[q] = g1send[q]
    for x2, y2, c2, where in cross:
        send(g1send.at[x2 * 8 + y2 * 2 + c2], g1recv.at[q], where, 8)
    for row in range(8):
        mixed[32 * row : 32 * row + 32] = dot(mix_in[...], gpre[32 * row : 32 * row + 32], (1, 0))

    analysis_middle(1)

    arrived(g1recv, 31, 8)
    total = g1recv[0]
    for i in range(1, 32):
        total = total + g1recv[i]
    g2send[...] = total
    g2recv[z] = total
    for z2, where in ring:
        send(g2send, g2recv.at[z], where, 9)

    adjoint = analysis_end(1)
    modes = dot(paired(adjoint, 1.0, -1.0), wcat[...], (1, 1))
    synthesis_start(modes, 1)

    arrived(g2recv, 15, 9)
    total = g2recv[0]
    for i in range(1, 16):
        total = total + g2recv[i]
    g3recv[q] = total
    for x2, y2, c2, where in cross:
        send(g3recv.at[q], g3recv.at[q], where, 10)

    for j4 in range(4):
        arow[4 * j4 : 4 * j4 + 4] = adjoint[:, 32 * j4 : 32 * j4 + 32]
    rows = lax.broadcasted_iota(jnp.int32, (16, 128), 0)
    lanes = lax.broadcasted_iota(jnp.int32, (16, 128), 1)
    diagonal = rows // 4 == lanes // 32
    targets = arow[...].astype(BF)
    part = lax.rem(rows, 4)
    for k2 in range(2):
        real = jnp.broadcast_to(spectrum[k2 : k2 + 1], (16, 128))
        imag = jnp.broadcast_to(spectrum[2 + k2 : 3 + k2], (16, 128))
        for r in range(2):
            on_real = real if r == 0 else -imag
            on_imag = imag if r == 0 else real
            left = jnp.where(part == k2, on_real, jnp.where(part == 2 + k2, on_imag, 0.0))
            left = jnp.where(diagonal, left, 0.0).astype(BF)
            product = dot(left, targets, (0, 0))
            for j4 in range(4):
                spec_s[j4, k2, r] = product[32 * j4 : 32 * j4 + 32]
    stores.append(pltpu.make_async_copy(spec_s, spec_out, out_sem.at[1]))
    stores[1].start()

    synthesis_middle(1)

    arrived(g3recv, 31, 10)
    for i in range(16):
        headg_s[2 * i : 2 * i + 2] = g3recv[i]
    for i in range(4):
        rows2 = g3recv[16 + i]
        for j in range(4):
            mixg_s[8 * j + 2 * i : 8 * j + 2 * i + 2] = rows2[:, 32 * j : 32 * j + 32]
    stores.append(pltpu.make_async_copy(mixg_s, mixg_out, out_sem.at[2]))
    stores.append(pltpu.make_async_copy(headg_s, headg_out, out_sem.at[3]))
    stores[2].start()
    stores[3].start()

    field = synthesis_end(0, 1) + mixed[...]
    for row in range(8):
        fin[pl.ds(row, 32, stride=8), :] = field[32 * row : 32 * row + 32]
    field_s[...] = fin[...].astype(BF)
    stores.append(pltpu.make_async_copy(field_s, field_out, out_sem.at[4]))
    stores[4].start()

    for turn in range(2):
        sent(arecv.at[turn], 31, 4 * turn)
        sent(brecv.at[turn], 15, 4 * turn + 1)
        sent(crecv.at[turn], 15, 4 * turn + 2)
        sent(drecv.at[turn], 31, 4 * turn + 3)
    sent(g1recv, 31, 8)
    sent(g2recv, 15, 9)
    sent(g3recv, 31, 10)
    for store in stores:
        store.wait()


def body(lifted_field, spectral_weight, mix_weight, mix_bias, head_weight, head_bias, out_weight, cotangent):
    forward_z, inverse_z = z_tables()
    forward_x, inverse_x = x_tables()
    inputs = (
        lifted_field.reshape(256, 128), spectral_weight, mix_weight, mix_bias.reshape(1, 32), head_weight,
        head_bias.reshape(1, 128), out_weight.reshape(1, 128), cotangent.reshape(8, 128),
        jnp.asarray(forward_z), jnp.asarray(inverse_z), jnp.asarray(y_tables()), jnp.asarray(forward_x), jnp.asarray(inverse_x),
    )
    whole = lambda a: pltpu.VMEM(a.shape, a.dtype)
    tail = lambda a: pltpu.VMEM(a.shape[1:], a.dtype)
    outputs = [
        jax.ShapeDtypeStruct((8, 128), F32), jax.ShapeDtypeStruct((256, 128), BF),
        jax.ShapeDtypeStruct((4, 2, 2, 32, 32), F32), jax.ShapeDtypeStruct((32, 32), F32), jax.ShapeDtypeStruct((32, 128), F32),
    ]
    scratch = [whole(a) for a in inputs[:10]] + [tail(a) for a in inputs[10:]] + [pltpu.VMEM((512, 512), BF)]
    scratch += [
        pltpu.VMEM((256, 128), F32), pltpu.VMEM((256, 128), BF), pltpu.VMEM((512, 128), BF), pltpu.VMEM((128, 512), BF),
        pltpu.VMEM((256, 128), F32), pltpu.VMEM((256, 128), BF), pltpu.VMEM((256, 128), F32), pltpu.VMEM((1024, 128), BF),
        pltpu.VMEM((256, 128), BF), pltpu.VMEM((256, 128), F32), pltpu.VMEM((32, 512), F32), pltpu.VMEM((64, 128), F32),
        pltpu.VMEM((8, 128), F32), pltpu.VMEM((16, 32), F32),
    ]
    scratch += [whole(a) for a in outputs]
    scratch += [
        pltpu.VMEM((2, 8, 16, 128), BF), pltpu.VMEM((2, 32, 16, 128), BF),
        pltpu.VMEM((2, 16, 4, 128), F32), pltpu.VMEM((2, 16, 4, 128), F32),
        pltpu.VMEM((2, 4, 128), F32), pltpu.VMEM((2, 16, 4, 128), F32),
        pltpu.VMEM((2, 8, 16, 128), BF), pltpu.VMEM((2, 32, 16, 128), BF),
        pltpu.VMEM((32, 2, 128), F32), pltpu.VMEM((32, 2, 128), F32),
        pltpu.VMEM((2, 128), F32), pltpu.VMEM((16, 2, 128), F32), pltpu.VMEM((32, 2, 128), F32),
        pltpu.SemaphoreType.DMA((13,)), pltpu.SemaphoreType.DMA((5,)), pltpu.SemaphoreType.DMA((11,)), pltpu.SemaphoreType.DMA((11,)),
    ]
    prediction, field, spectral, mix_grad, head_grad = pl.pallas_call(
        kernel,
        out_shape=outputs,
        in_specs=[pl.BlockSpec(memory_space=pltpu.HBM)] * len(inputs),
        out_specs=[pl.BlockSpec(memory_space=pltpu.HBM)] * len(outputs),
        scratch_shapes=scratch,
        name="step",
        compiler_params=pltpu.CompilerParams(collective_id=0, has_side_effects=True),
    )(*inputs)
    return prediction.reshape(1, 8, 128), field.reshape(1, 32, 8, 128), spectral, mix_grad, head_grad


def solution(mesh):
    return jax.shard_map(
        body,
        mesh=mesh,
        in_specs=(
            P("wide", None, "narrow", None),
            P("wide", "narrow", None, None, None),
            P(),
            P(),
            P(),
            P(),
            P(),
            P("wide", "narrow", None),
        ),
        out_specs=(
            P("wide", "narrow", None),
            P("wide", None, "narrow", None),
            P("wide", "narrow", None, None, None),
            P(),
            P(),
        ),
        check_vma=False,
    )
```

time: 2010 us -> 76.3 us (0.04)
  waiting for transfers between devices: 1580 us -> 0 us
  blocking collectives: 347 us -> 0 us
  Pallas kernels: 0 us -> 69.6 us
  starting transfers between devices: 35.3 us -> 0 us
    unnamed x4 -> x0, waiting for transfers between devices: 1530 us -> none
    all_gather x2 -> x0, blocking collectives: 246 us -> none  [synthesis(): shard_piece = lax.all_gather(spectrum, 'wide', axis=0, tiled=True)]
    psum x1 -> x0, blocking collectives: 101 us -> none  [body(): lax.psum((mix_terms, jnp.sum(head_parts, axis=0)), ('wide', 'narrow'))]
    pallas_call x0 -> x1, Pallas kernels: none -> 69.6 us  [body(): pl.pallas_call(kernel, out_shape=outputs, in_specs=[pl.BlockSpec(memory_s...]
    all_to_all x4 -> x0, waiting for transfers between devices: 52.4 us -> none  [the longest x2 26.3 us: analysis(): lax.all_to_all(spectra, 'narrow', split_axis=0, concat_axis=4, tiled=True)]
    all_to_all x4 -> x0, starting transfers between devices: 35.2 us -> none  [the longest x2 21.4 us: analysis(): lax.all_to_all(spectra, 'narrow', split_axis=0, concat_axis=4, tiled=True)]
  transfers between devices with their start and end apart: 6 -> 0, of which waited for: 6 -> 0; matrix products, arithmetic and copies ran while one was open for 0% -> 0% of each run, Pallas kernels for 0% -> 0%
where the time goes in v1:
time: 76.3 us; the launch traced here: 76 us
  Pallas kernels  69.6 us (91%)
  local copies, waits for them, and re-layouts  5.76 us (8%)
    pallas_call x1, Pallas kernels, body(): pl.pallas_call(kernel, out_shape=outputs, in_specs=[pl.BlockSpec(memory_s...  69.6 us
    unnamed x11, local copies, waits for them, and re-layouts  5.76 us

profile of v1, /device:TPU:1, one launch (start us, length us, event | category | flops | bytes accessed | tf_op | source)
XLA Modules:
  0.0 76.0 jit_solution(6424529553542370267)
XLA Ops:
  0.6 69.6 %step.1 = (f32[8,128]{1,0:T(8,128)}, bf16[256,128]{1,0:T(8,128)(2,1)}, f32[4,2,2,32,32]{4,3,2,1,0:T(8,128)}, f32[32,32]{1,0:T(8,128)}, f32[32,128]{1,0:T(8,128)}) custom-call(bf16[256,128]{1,0:T(8,128)(2,1)} %bitcast.7, f32[4,2,2,32,32]{4,3,2,1,0:T(8,128)} %w_hbm.1, bf16[32,32]{1,0:T(8,128)(2,1)} %mix_hbm.1, f32[1,32]{1,0:T(1,128)} %bitcast.11, ...), custom_call_target="tpu_custom_call" | custom-call | tf_op jit(solution)/shard_map/step/pallas_call | solution.py:408
  70.3 0.0 copy-start.2
  70.3 0.7 copy-done.2
  71.0 0.6 copy.23
  71.6 1.5 %copy.24 = bf16[1,32,8,128]{3,2,1,0:T(8,128)(2,1)} copy(bf16[1,32,8,128]{3,2,1,0:T(8,128)(2,1)} %bitcast.8) | data formatting | bytes 131072
  73.0 0.0 copy-start.1
  73.0 1.7 %copy.25 = f32[4,2,2,32,32]{4,3,2,1,0:T(8,128)} copy(f32[4,2,2,32,32]{4,3,2,1,0:T(8,128)} %get-tuple-element.22) | data formatting | bytes 131072
  74.7 0.0 copy-done.1
  74.7 0.0 copy-start
  74.7 0.6 copy.26
  75.3 0.1 copy-done
  75.4 0.6 copy.27
Async XLA Ops:
  70.3 0.7 copy-start.2
  73.0 1.7 %copy-start.1 = (f32[32,32]{1,0:T(8,128)S(1)}, f32[32,32]{1,0:T(8,128)}, u32[]{:S(2)}) copy-start(f32[32,32]{1,0:T(8,128)} %get-tuple-element.23) | copy-start | bytes 12292
  74.7 0.7 copy-start

commit v2 on v1

--- a/solution.py
+++ b/solution.py
@@ -63,8 +63,8 @@
 
 @functools.lru_cache(None)
 def x_tables():
-    forward = np.zeros((4, 8, 16, 2, 2, 4, 2, 2, 2, 4), np.float32)
-    inverse = np.zeros((4, 8, 16, 2, 2, 4, 2, 2, 2, 4), np.float32)
+    forward = np.zeros((4, 8, 4, 4, 2, 2, 4, 2, 2, 2, 4), np.float32)
+    inverse = np.zeros((4, 8, 4, 4, 2, 2, 4, 2, 2, 2, 4), np.float32)
     for y in range(4):
         for zl in range(8):
             for i4 in range(4):
@@ -75,11 +75,11 @@
                         for par in range(2):
                             for zh in range(2):
                                 for k2 in range(2):
-                                    z2, kk = zh * 8 + 2 * i4 + par, 2 * zh + k2
+                                    kk, kind, block = 2 * zh + k2, (2 * i4 + par) % 4, 2 * zh + i4 // 2
                                     for s, t, value in ((0, 0, co), (0, 1, si), (1, 0, -si), (1, 1, co)):
-                                        forward[y, zl, z2, s, k2, y2, c2, par, t, kk] = value
+                                        forward[y, zl, kind, block, s, k2, y2, c2, par, t, kk] = value
                                     for s, t, value in ((0, 0, co), (0, 1, -si), (1, 0, si), (1, 1, co)):
-                                        inverse[y, zl, z2, t, k2, y2, c2, par, s, kk] = value
+                                        inverse[y, zl, kind, block, t, k2, y2, c2, par, s, kk] = value
     return narrow_type(forward.reshape(32, 64, 128)), narrow_type(inverse.reshape(32, 64, 128))
 
 
@@ -101,11 +101,10 @@
     v_hbm, w_hbm, mix_hbm, bias_hbm, head_hbm, hb_hbm, ow_hbm, cot_hbm, ez_hbm, ei_hbm, r_hbm, t1_hbm, t2_hbm,
     pred_out, field_out, spec_out, mixg_out, headg_out,
     v_in, w_in, mix_in, bias_in, head_in, hb_in, ow_in, cot_in, ez_in, ei_in, r_rows, t1_in, t2_in, r_in,
-    vf, vy, wst, wcat, mixed, hidden, gp, slope, gpre, fin, lhs, zrow, srow, arow,
-    pred_s, field_s, spec_s, mixg_s, headg_s,
-    asend, arecv, bsend, brecv, csend, crecv, dsend, drecv,
+    vf, vy, wflat, wall, wst, wcat, mixed, hidden, gp, slope, gpre, fin, lhs, srow, arow, own,
+    asend, arecv, bsend, brecv, crecv, dsend, drecv,
     g1send, g1recv, g2send, g2recv, g3recv,
-    in_sem, out_sem, send_sem, recv_sem,
+    in_sem, send_sem, recv_sem,
 ):
     w = lax.axis_index("wide")
     n = lax.axis_index("narrow")
@@ -113,6 +112,7 @@
     x, zh = n // 2, lax.rem(n, 2)
     q = x * 8 + y * 2 + c
     z = zh * 8 + zl
+    kind, block = lax.rem(zl, 4), 2 * zh + zl // 4
 
     cross = []
     for dx, dy, dc in CROSS:
@@ -122,6 +122,8 @@
     for d in RING:
         z2 = lax.rem(z + d, 16)
         ring.append((z2, (y * 16 + lax.rem(z2, 8) * 2 + c, x * 2 + z2 // 8)))
+    near = [ring[RING.index(d)][1] for d in (14, 1, 15)]
+    alike = [ring[RING.index(d)][1] for d in (8, 4, 12)]
 
     barrier = pltpu.get_barrier_semaphore()
     for *_, where in ring:
@@ -171,43 +173,43 @@
         arrived(arecv.at[turn], 31, 4 * turn)
         table = t1_in[...]
         table = jnp.concatenate([table] * 4, axis=1)
-        partial = dot(table, arecv[turn].reshape(512, 128), (1, 0))
-        for z2 in range(16):
-            bsend[turn, z2] = partial[4 * z2 : 4 * z2 + 4]
-        brecv[turn, z] = bsend[turn, z]
+        partial = dot(table, arecv[turn].reshape(512, 128), (1, 0)).astype(BF)
+        for piece in range(4):
+            bsend[turn, piece] = partial[16 * piece : 16 * piece + 16]
+        brecv[turn, z] = bsend[turn, kind]
         for z2, where in ring:
-            send(bsend.at[turn, z2], brecv.at[turn, z], where, 4 * turn + 1)
+            send(bsend.at[turn, lax.rem(z2, 4)], brecv.at[turn, z], where, 4 * turn + 1)
 
     def analysis_end(turn):
         arrived(brecv.at[turn], 15, 4 * turn + 1)
-        total = brecv[turn, 0]
+        total = brecv[turn, 0].astype(F32)
         for z2 in range(1, 16):
-            total = total + brecv[turn, z2]
+            total = total + brecv[turn, z2].astype(F32)
+        for i in range(4):
+            own[turn, i] = total[4 * i : 4 * i + 4]
         return total
 
     def paired(spectrum, low_sign, high_sign):
-        srow[0:2] = low_sign * spectrum[2:4]
-        srow[2:4] = high_sign * spectrum[0:2]
-        turned = srow[0:4]
-        row = lax.broadcasted_iota(jnp.int32, (4, 128), 0)
-        even = lax.rem(row, 2) == 0
-        parts = [
-            jnp.where(even, spectrum, 0.0), jnp.where(even, turned, 0.0),
-            jnp.where(even, 0.0, spectrum), jnp.where(even, 0.0, turned),
-        ]
+        for i in range(4):
+            srow[4 * i : 4 * i + 2] = low_sign * spectrum[4 * i + 2 : 4 * i + 4]
+            srow[4 * i + 2 : 4 * i + 4] = high_sign * spectrum[4 * i : 4 * i + 2]
+        turned = srow[...]
+        row = lax.broadcasted_iota(jnp.int32, (16, 128), 0)
+        parts = []
+        for i in range(4):
+            for k2 in range(2):
+                mine = (row // 4 == i) & (lax.rem(row, 2) == k2)
+                parts += [jnp.where(mine, spectrum, 0.0), jnp.where(mine, turned, 0.0)]
         return jnp.concatenate(parts, axis=1).astype(BF)
 
     def synthesis_start(modes, turn):
-        csend[turn] = modes
-        crecv[turn, z] = modes
-        for z2, where in ring:
-            send(csend.at[turn], crecv.at[turn, z], where, 4 * turn + 2)
+        crecv[turn, kind] = modes.astype(BF)
+        for where in near:
+            send(crecv.at[turn, kind], crecv.at[turn, kind], where, 4 * turn + 2)
 
     def synthesis_middle(turn):
-        arrived(crecv.at[turn], 15, 4 * turn + 2)
-        for z2 in range(16):
-            zrow[4 * z2 : 4 * z2 + 4] = crecv[turn, z2]
-        planes = dot(t2_in[...], zrow[...].astype(BF), (0, 0)).astype(BF)
+        arrived(crecv.at[turn], 3, 4 * turn + 2)
+        planes = dot(t2_in[...], crecv[turn].reshape(64, 128), (0, 0)).astype(BF)
         for piece in range(8):
             dsend[turn, piece] = planes[16 * piece : 16 * piece + 16]
         drecv[turn, q] = dsend[turn, y * 2 + c]
@@ -240,15 +242,12 @@
 
     for load in loads[3:]:
         load.wait()
-    for k2 in range(2):
-        for r in range(2):
-            for j4 in range(4):
-                block = w_in[j4, k2, r].astype(BF)
-                zero = jnp.zeros((32, 32), BF)
-                wide = jnp.concatenate([zero] * j4 + [block] + [zero] * (3 - j4), axis=1)
-                base = 128 * (2 * k2 + r)
-                wst[base + 32 * j4 : base + 32 * j4 + 32] = wide
-                wcat[32 * j4 : 32 * j4 + 32, base : base + 128] = wide
+    for j4 in range(4):
+        for k2 in range(2):
+            for r in range(2):
+                base = 128 * (2 * k2 + r) + 32 * j4
+                wflat[:, base : base + 32] = w_in[j4, k2, r]
+    wall[block] = wflat[...].astype(BF)
     bias_col = column(bias_in[...], 32)
     for row in range(8):
         mixed[32 * row : 32 * row + 32] = dot(mix_in[...], vy[32 * row : 32 * row + 32], (0, 0)) + bias_col
@@ -257,9 +256,19 @@
 
     pl.semaphore_wait(barrier, len(CROSS) + len(RING))
     analysis_send(0)
+    for where in alike:
+        send(wall.at[block], wall.at[block], where, 11)
     analysis_middle(0)
-    spectrum = analysis_end(0)
-    modes = dot(paired(spectrum, -1.0, 1.0), wst[...], (1, 0))
+    arrived(wall, 3, 11)
+    inside = lax.broadcasted_iota(jnp.int32, (128, 128), 0) // 32 == lax.broadcasted_iota(jnp.int32, (128, 128), 1) // 32
+    for i in range(4):
+        for part in range(4):
+            compact = wall[i, :, 128 * part : 128 * part + 128].astype(F32)
+            full = jnp.where(inside, jnp.concatenate([compact] * 4, axis=0), 0.0).astype(BF)
+            base = 128 * (4 * i + part)
+            wst[base : base + 128] = full
+            wcat[:, base : base + 128] = full
+    modes = dot(paired(analysis_end(0), -1.0, 1.0), wst[...], (1, 0))
     synthesis_start(modes, 0)
     synthesis_middle(0)
     pre = synthesis_end(1, 0) + mixed[...]
@@ -270,12 +279,10 @@
     for row in range(8):
         head_pre = dot(head_in[...], hidden[32 * row : 32 * row + 32], (0, 0)) + head_col
         value, rate = gelu_parts(head_pre)
-        pred_s[row : row + 1] = dot(ow_in[...], value.astype(BF), (1, 0))
+        pred_out[row : row + 1] = dot(ow_in[...], value.astype(BF), (1, 0))
         slope[128 * row : 128 * row + 128] = (cot_in[row : row + 1] * out_col * rate).astype(BF)
         back = dot(head_in[...], slope[128 * row : 128 * row + 128], (1, 0))
         gpre[32 * row : 32 * row + 32] = (back * gp[32 * row : 32 * row + 32]).astype(BF)
-    stores = [pltpu.make_async_copy(pred_s, pred_out, out_sem.at[0])]
-    stores[0].start()
     local_analysis(gpre[...], 1, 1)
     analysis_send(1)
 
@@ -308,9 +315,10 @@
     for z2, where in ring:
         send(g2send, g2recv.at[z], where, 9)
 
-    adjoint = analysis_end(1)
-    modes = dot(paired(adjoint, 1.0, -1.0), wcat[...], (1, 1))
+    modes = dot(paired(analysis_end(1), 1.0, -1.0), wcat[...], (1, 1))
     synthesis_start(modes, 1)
+    spectrum = own[0, block]
+    adjoint = own[1, block]
 
     arrived(g2recv, 15, 9)
     total = g2recv[0]
@@ -337,41 +345,41 @@
             left = jnp.where(diagonal, left, 0.0).astype(BF)
             product = dot(left, targets, (0, 0))
             for j4 in range(4):
-                spec_s[j4, k2, r] = product[32 * j4 : 32 * j4 + 32]
-    stores.append(pltpu.make_async_copy(spec_s, spec_out, out_sem.at[1]))
-    stores[1].start()
+                spec_out[j4, k2, r] = product[32 * j4 : 32 * j4 + 32]
 
     synthesis_middle(1)
 
     arrived(g3recv, 31, 10)
     for i in range(16):
-        headg_s[2 * i : 2 * i + 2] = g3recv[i]
+        headg_out[2 * i : 2 * i + 2] = g3recv[i]
     for i in range(4):
         rows2 = g3recv[16 + i]
         for j in range(4):
-            mixg_s[8 * j + 2 * i : 8 * j + 2 * i + 2] = rows2[:, 32 * j : 32 * j + 32]
-    stores.append(pltpu.make_async_copy(mixg_s, mixg_out, out_sem.at[2]))
-    stores.append(pltpu.make_async_copy(headg_s, headg_out, out_sem.at[3]))
-    stores[2].start()
-    stores[3].start()
+            mixg_out[8 * j + 2 * i : 8 * j + 2 * i + 2] = rows2[:, 32 * j : 32 * j + 32]
 
     field = synthesis_end(0, 1) + mixed[...]
     for row in range(8):
         fin[pl.ds(row, 32, stride=8), :] = field[32 * row : 32 * row + 32]
-    field_s[...] = fin[...].astype(BF)
-    stores.append(pltpu.make_async_copy(field_s, field_out, out_sem.at[4]))
-    stores[4].start()
+    field_out[...] = fin[...].astype(BF)
 
     for turn in range(2):
         sent(arecv.at[turn], 31, 4 * turn)
         sent(brecv.at[turn], 15, 4 * turn + 1)
-        sent(crecv.at[turn], 15, 4 * turn + 2)
+        sent(crecv.at[turn], 3, 4 * turn + 2)
         sent(drecv.at[turn], 31, 4 * turn + 3)
     sent(g1recv, 31, 8)
     sent(g2recv, 15, 9)
     sent(g3recv, 31, 10)
-    for store in stores:
-        store.wait()
+    sent(wall, 3, 11)
+
+
+def publish(*refs):
+    sem = refs[-1]
+    copies = [pltpu.make_async_copy(refs[i], refs[5 + i], sem.at[i]) for i in (2, 1, 0, 3, 4)]
+    for copy in copies:
+        copy.start()
+    for copy in copies:
+        copy.wait()
 
 
 def body(lifted_field, spectral_weight, mix_weight, mix_bias, head_weight, head_bias, out_weight, cotangent):
@@ -382,6 +390,7 @@
         head_bias.reshape(1, 128), out_weight.reshape(1, 128), cotangent.reshape(8, 128),
         jnp.asarray(forward_z), jnp.asarray(inverse_z), jnp.asarray(y_tables()), jnp.asarray(forward_x), jnp.asarray(inverse_x),
     )
+    inputs = tuple(pltpu.with_memory_space_constraint(a, pltpu.HBM) for a in inputs)
     whole = lambda a: pltpu.VMEM(a.shape, a.dtype)
     tail = lambda a: pltpu.VMEM(a.shape[1:], a.dtype)
     outputs = [
@@ -390,30 +399,38 @@
     ]
     scratch = [whole(a) for a in inputs[:10]] + [tail(a) for a in inputs[10:]] + [pltpu.VMEM((512, 512), BF)]
     scratch += [
-        pltpu.VMEM((256, 128), F32), pltpu.VMEM((256, 128), BF), pltpu.VMEM((512, 128), BF), pltpu.VMEM((128, 512), BF),
+        pltpu.VMEM((256, 128), F32), pltpu.VMEM((256, 128), BF), pltpu.VMEM((32, 512), F32), pltpu.VMEM((4, 32, 512), BF),
+        pltpu.VMEM((2048, 128), BF), pltpu.VMEM((128, 2048), BF),
         pltpu.VMEM((256, 128), F32), pltpu.VMEM((256, 128), BF), pltpu.VMEM((256, 128), F32), pltpu.VMEM((1024, 128), BF),
-        pltpu.VMEM((256, 128), BF), pltpu.VMEM((256, 128), F32), pltpu.VMEM((32, 512), F32), pltpu.VMEM((64, 128), F32),
-        pltpu.VMEM((8, 128), F32), pltpu.VMEM((16, 32), F32),
+        pltpu.VMEM((256, 128), BF), pltpu.VMEM((256, 128), F32), pltpu.VMEM((32, 512), F32),
+        pltpu.VMEM((16, 128), F32), pltpu.VMEM((16, 32), F32), pltpu.VMEM((2, 4, 4, 128), F32),
     ]
-    scratch += [whole(a) for a in outputs]
     scratch += [
         pltpu.VMEM((2, 8, 16, 128), BF), pltpu.VMEM((2, 32, 16, 128), BF),
-        pltpu.VMEM((2, 16, 4, 128), F32), pltpu.VMEM((2, 16, 4, 128), F32),
-        pltpu.VMEM((2, 4, 128), F32), pltpu.VMEM((2, 16, 4, 128), F32),
+        pltpu.VMEM((2, 4, 16, 128), BF), pltpu.VMEM((2, 16, 16, 128), BF), pltpu.VMEM((2, 4, 16, 128), BF),
         pltpu.VMEM((2, 8, 16, 128), BF), pltpu.VMEM((2, 32, 16, 128), BF),
         pltpu.VMEM((32, 2, 128), F32), pltpu.VMEM((32, 2, 128), F32),
         pltpu.VMEM((2, 128), F32), pltpu.VMEM((16, 2, 128), F32), pltpu.VMEM((32, 2, 128), F32),
-        pltpu.SemaphoreType.DMA((13,)), pltpu.SemaphoreType.DMA((5,)), pltpu.SemaphoreType.DMA((11,)), pltpu.SemaphoreType.DMA((11,)),
+        pltpu.SemaphoreType.DMA((13,)), pltpu.SemaphoreType.DMA((12,)), pltpu.SemaphoreType.DMA((12,)),
     ]
-    prediction, field, spectral, mix_grad, head_grad = pl.pallas_call(
+    results = pl.pallas_call(
         kernel,
         out_shape=outputs,
         in_specs=[pl.BlockSpec(memory_space=pltpu.HBM)] * len(inputs),
-        out_specs=[pl.BlockSpec(memory_space=pltpu.HBM)] * len(outputs),
+        out_specs=[pl.BlockSpec(memory_space=pltpu.VMEM)] * len(outputs),
         scratch_shapes=scratch,
         name="step",
-        compiler_params=pltpu.CompilerParams(collective_id=0, has_side_effects=True),
+        compiler_params=pltpu.CompilerParams(collective_id=0, has_side_effects=True, vmem_limit_bytes=32 << 20),
     )(*inputs)
+    prediction, field, spectral, mix_grad, head_grad = pl.pallas_call(
+        publish,
+        out_shape=outputs,
+        in_specs=[pl.BlockSpec(memory_space=pltpu.VMEM)] * len(outputs),
+        out_specs=[pl.BlockSpec(memory_space=pltpu.HBM)] * len(outputs),
+        scratch_shapes=[pltpu.SemaphoreType.DMA((5,))],
+        name="publish",
+        compiler_params=pltpu.CompilerParams(vmem_limit_bytes=4 << 20),
+    )(*results)
     return prediction.reshape(1, 8, 128), field.reshape(1, 32, 8, 128), spectral, mix_grad, head_grad
 
 

time: 76.3 us -> 66.5 us (0.87)
  local copies, waits for them, and re-layouts: 5.76 us -> 0 us
  Pallas kernels: 69.6 us -> 65.7 us
    unnamed x11 -> x0, local copies, waits for them, and re-layouts: 5.76 us -> none
    pallas_call x1, Pallas kernels: 69.6 us -> 64.9 us  [body(): pl.pallas_call(kernel, out_shape=outputs, in_specs=[pl.BlockSpec(memory_s...]
    pallas_call x0 -> x1, Pallas kernels: none -> 0.77 us  [body(): pl.pallas_call(publish, out_shape=outputs, in_specs=[pl.BlockSpec(memory_...]
where the time goes in v2:
time: 66.5 us; the launch traced here: 66.3 us
  Pallas kernels  65.7 us (99%)
    pallas_call x1, Pallas kernels, body(): pl.pallas_call(kernel, out_shape=outputs, in_specs=[pl.BlockSpec(memory_s...  64.9 us

profile of v2, /device:TPU:1, one launch (start us, length us, event | category | flops | bytes accessed | tf_op | source)
XLA Modules:
  0.0 66.3 jit_solution(18370388667436954516)
XLA Ops:
  0.6 64.9 %step.1 = (f32[8,128]{1,0:T(8,128)S(1)}, bf16[256,128]{1,0:T(8,128)(2,1)S(1)}, f32[4,2,2,32,32]{4,3,2,1,0:T(8,128)S(1)}, f32[32,32]{1,0:T(8,128)S(1)}, f32[32,128]{1,0:T(8,128)S(1)}) custom-call(bf16[256,128]{1,0:T(8,128)(2,1)} %bitcast.7, f32[4,2,2,32,32]{4,3,2,1,0:T(8,128)} %w_hbm.1, bf16[32,32]{1,0:T(8,128)(2,1)} %mix_hbm.1, f32[1,32]{1,0:T(1,128)} %bitcast.9, ...), custom_call_target="tpu_custom_call" | custom-call | tf_op jit(solution)/shard_map/step/pallas_call | solution.py:416
  65.6 0.8 %publish.1 = (f32[8,128]{1,0:T(8,128)}, bf16[256,128]{1,0:T(8,128)(2,1)}, f32[4,2,2,32,32]{4,3,2,1,0:T(8,128)}, f32[32,32]{1,0:T(8,128)}, f32[32,128]{1,0:T(8,128)}) custom-call(f32[8,128]{1,0:T(8,128)S(1)} %get-tuple-element.15.refs_0_, bf16[256,128]{1,0:T(8,128)(2,1)S(1)} %get-tuple-element.16.refs_1_, f32[4,2,2,32,32]{4,3,2,1,0:T(8,128)S(1)} %get-tuple-element.17.refs_2_, ...), custom_call_target="tpu_custom_call" | custom-call | tf_op jit(solution)/shard_map/publish/pallas_call | solution.py:425

commit v3 on v2

--- a/solution.py
+++ b/solution.py
@@ -104,7 +104,7 @@
     vf, vy, wflat, wall, wst, wcat, mixed, hidden, gp, slope, gpre, fin, lhs, srow, arow, own,
     asend, arecv, bsend, brecv, crecv, dsend, drecv,
     g1send, g1recv, g2send, g2recv, g3recv,
-    in_sem, send_sem, recv_sem,
+    in_sem, send_sem, recv_sem, passed,
 ):
     w = lax.axis_index("wide")
     n = lax.axis_index("narrow")
@@ -126,9 +126,8 @@
     alike = [ring[RING.index(d)][1] for d in (8, 4, 12)]
 
     barrier = pltpu.get_barrier_semaphore()
-    for *_, where in ring:
-        pl.semaphore_signal(barrier, inc=1, device_id=where, device_id_type=MESH)
-    for *_, where in cross:
+    close = [where for d, (_, where) in zip(RING, ring) if min(d, 16 - d) <= 4]
+    for where in close + [item[-1] for item in cross]:
         pl.semaphore_signal(barrier, inc=1, device_id=where, device_id_type=MESH)
 
     variant = y * 8 + zl
@@ -254,10 +253,14 @@
     head_col = column(hb_in[...], 128)
     out_col = column(ow_in[...].astype(F32), 128)
 
-    pl.semaphore_wait(barrier, len(CROSS) + len(RING))
+    pl.semaphore_wait(barrier, len(cross) + len(close))
+    for where in alike[1:]:
+        pl.semaphore_signal(passed, inc=1, device_id=where, device_id_type=MESH)
+    for where in alike[1:]:
+        send(wall.at[block], wall.at[block], where, 11)
     analysis_send(0)
-    for where in alike:
-        send(wall.at[block], wall.at[block], where, 11)
+    pl.semaphore_wait(passed, 2)
+    send(wall.at[block], wall.at[block], alike[0], 11)
     analysis_middle(0)
     arrived(wall, 3, 11)
     inside = lax.broadcasted_iota(jnp.int32, (128, 128), 0) // 32 == lax.broadcasted_iota(jnp.int32, (128, 128), 1) // 32
@@ -411,7 +414,7 @@
         pltpu.VMEM((2, 8, 16, 128), BF), pltpu.VMEM((2, 32, 16, 128), BF),
         pltpu.VMEM((32, 2, 128), F32), pltpu.VMEM((32, 2, 128), F32),
         pltpu.VMEM((2, 128), F32), pltpu.VMEM((16, 2, 128), F32), pltpu.VMEM((32, 2, 128), F32),
-        pltpu.SemaphoreType.DMA((13,)), pltpu.SemaphoreType.DMA((12,)), pltpu.SemaphoreType.DMA((12,)),
+        pltpu.SemaphoreType.DMA((13,)), pltpu.SemaphoreType.DMA((12,)), pltpu.SemaphoreType.DMA((12,)), pltpu.SemaphoreType.REGULAR,
     ]
     results = pl.pallas_call(
         kernel,

time: 66.5 us -> 63.9 us (0.961)
  Pallas kernels: 65.7 us -> 63.2 us
    pallas_call x1, Pallas kernels: 64.9 us -> 62.4 us  [body(): pl.pallas_call(kernel, out_shape=outputs, in_specs=[pl.BlockSpec(memory_s...]
where the time goes in v3:
time: 63.9 us; the launch traced here: 63.8 us
  Pallas kernels  63.2 us (99%)
  between operations  0.64 us (1%)
    pallas_call x1, Pallas kernels, body(): pl.pallas_call(kernel, out_shape=outputs, in_specs=[pl.BlockSpec(memory_s...  62.4 us

profile of v3, /device:TPU:1, one launch (start us, length us, event | category | flops | bytes accessed | tf_op | source)
XLA Modules:
  0.0 63.8 jit_solution(2847645716832711227)
XLA Ops:
  0.6 62.4 %step.1 = (f32[8,128]{1,0:T(8,128)S(1)}, bf16[256,128]{1,0:T(8,128)(2,1)S(1)}, f32[4,2,2,32,32]{4,3,2,1,0:T(8,128)S(1)}, f32[32,32]{1,0:T(8,128)S(1)}, f32[32,128]{1,0:T(8,128)S(1)}) custom-call(bf16[256,128]{1,0:T(8,128)(2,1)} %bitcast.7, f32[4,2,2,32,32]{4,3,2,1,0:T(8,128)} %w_hbm.1, bf16[32,32]{1,0:T(8,128)(2,1)} %mix_hbm.1, f32[1,32]{1,0:T(1,128)} %bitcast.9, ...), custom_call_target="tpu_custom_call" | custom-call | tf_op jit(solution)/shard_map/step/pallas_call | solution.py:419
  63.0 0.8 %publish.1 = (f32[8,128]{1,0:T(8,128)}, bf16[256,128]{1,0:T(8,128)(2,1)}, f32[4,2,2,32,32]{4,3,2,1,0:T(8,128)}, f32[32,32]{1,0:T(8,128)}, f32[32,128]{1,0:T(8,128)}) custom-call(f32[8,128]{1,0:T(8,128)S(1)} %get-tuple-element.15.refs_0_, bf16[256,128]{1,0:T(8,128)(2,1)S(1)} %get-tuple-element.16.refs_1_, f32[4,2,2,32,32]{4,3,2,1,0:T(8,128)S(1)} %get-tuple-element.17.refs_2_, ...), custom_call_target="tpu_custom_call" | custom-call | tf_op jit(solution)/shard_map/publish/pallas_call | solution.py:428

commit v4 on v3

--- a/solution.py
+++ b/solution.py
@@ -279,13 +279,20 @@
     value, rate = gelu_parts(pre)
     hidden[...] = value.astype(BF)
     gp[...] = rate
-    for row in range(8):
-        head_pre = dot(head_in[...], hidden[32 * row : 32 * row + 32], (0, 0)) + head_col
+    for first in range(0, 8, 2):
+        group = range(first, first + 2)
+        side = jnp.concatenate([hidden[32 * row : 32 * row + 32] for row in group], axis=1)
+        head_pre = dot(head_in[...], side, (0, 0)) + jnp.concatenate([head_col] * 2, axis=1)
         value, rate = gelu_parts(head_pre)
-        pred_out[row : row + 1] = dot(ow_in[...], value.astype(BF), (1, 0))
-        slope[128 * row : 128 * row + 128] = (cot_in[row : row + 1] * out_col * rate).astype(BF)
-        back = dot(head_in[...], slope[128 * row : 128 * row + 128], (1, 0))
-        gpre[32 * row : 32 * row + 32] = (back * gp[32 * row : 32 * row + 32]).astype(BF)
+        line = dot(ow_in[...], value.astype(BF), (1, 0))
+        drive = jnp.concatenate([cot_in[row : row + 1] * out_col for row in group], axis=1)
+        tilt = (drive * rate).astype(BF)
+        back = dot(head_in[...], tilt, (1, 0))
+        for i, row in enumerate(group):
+            lanes = slice(128 * i, 128 * i + 128)
+            pred_out[row : row + 1] = line[:, lanes]
+            slope[128 * row : 128 * row + 128] = tilt[:, lanes]
+            gpre[32 * row : 32 * row + 32] = (back[:, lanes] * gp[32 * row : 32 * row + 32]).astype(BF)
     local_analysis(gpre[...], 1, 1)
     analysis_send(1)
 
@@ -330,6 +337,8 @@
     g3recv[q] = total
     for x2, y2, c2, where in cross:
         send(g3recv.at[q], g3recv.at[q], where, 10)
+
+    synthesis_middle(1)
 
     for j4 in range(4):
         arow[4 * j4 : 4 * j4 + 4] = adjoint[:, 32 * j4 : 32 * j4 + 32]
@@ -349,8 +358,6 @@
             product = dot(left, targets, (0, 0))
             for j4 in range(4):
                 spec_out[j4, k2, r] = product[32 * j4 : 32 * j4 + 32]
-
-    synthesis_middle(1)
 
     arrived(g3recv, 31, 10)
     for i in range(16):

time: 63.9 us -> 63.1 us (0.987)
  Pallas kernels: 63.2 us -> 62.3 us
    pallas_call x1, Pallas kernels: 62.4 us -> 61.5 us  [body(): pl.pallas_call(kernel, out_shape=outputs, in_specs=[pl.BlockSpec(memory_s...]
where the time goes in v4:
time: 63.1 us; the launch traced here: 63 us
  Pallas kernels  62.3 us (99%)
  between operations  0.64 us (1%)
    pallas_call x1, Pallas kernels, body(): pl.pallas_call(kernel, out_shape=outputs, in_specs=[pl.BlockSpec(memory_s...  61.5 us

profile of v4, /device:TPU:1, one launch (start us, length us, event | category | flops | bytes accessed | tf_op | source)
XLA Modules:
  0.0 63.0 jit_solution(17748305560453789357)
XLA Ops:
  0.6 61.5 %step.1 = (f32[8,128]{1,0:T(8,128)S(1)}, bf16[256,128]{1,0:T(8,128)(2,1)S(1)}, f32[4,2,2,32,32]{4,3,2,1,0:T(8,128)S(1)}, f32[32,32]{1,0:T(8,128)S(1)}, f32[32,128]{1,0:T(8,128)S(1)}) custom-call(bf16[256,128]{1,0:T(8,128)(2,1)} %bitcast.7, f32[4,2,2,32,32]{4,3,2,1,0:T(8,128)} %w_hbm.1, bf16[32,32]{1,0:T(8,128)(2,1)} %mix_hbm.1, f32[1,32]{1,0:T(1,128)} %bitcast.9, ...), custom_call_target="tpu_custom_call" | custom-call | tf_op jit(solution)/shard_map/step/pallas_call | solution.py:426
  62.2 0.8 %publish.1 = (f32[8,128]{1,0:T(8,128)}, bf16[256,128]{1,0:T(8,128)(2,1)}, f32[4,2,2,32,32]{4,3,2,1,0:T(8,128)}, f32[32,32]{1,0:T(8,128)}, f32[32,128]{1,0:T(8,128)}) custom-call(f32[8,128]{1,0:T(8,128)S(1)} %get-tuple-element.15.refs_0_, bf16[256,128]{1,0:T(8,128)(2,1)S(1)} %get-tuple-element.16.refs_1_, f32[4,2,2,32,32]{4,3,2,1,0:T(8,128)S(1)} %get-tuple-element.17.refs_2_, ...), custom_call_target="tpu_custom_call" | custom-call | tf_op jit(solution)/shard_map/publish/pallas_call | solution.py:435

commit v5 on v4

--- a/solution.py
+++ b/solution.py
@@ -124,6 +124,8 @@
         ring.append((z2, (y * 16 + lax.rem(z2, 8) * 2 + c, x * 2 + z2 // 8)))
     near = [ring[RING.index(d)][1] for d in (14, 1, 15)]
     alike = [ring[RING.index(d)][1] for d in (8, 4, 12)]
+    up, down = lax.rem(z + 4, 16), lax.rem(z + 12, 16)
+    up, down = 2 * (up // 8) + lax.rem(up, 8) // 4, 2 * (down // 8) + lax.rem(down, 8) // 4
 
     barrier = pltpu.get_barrier_semaphore()
     close = [where for d, (_, where) in zip(RING, ring) if min(d, 16 - d) <= 4]
@@ -260,9 +262,12 @@
         send(wall.at[block], wall.at[block], where, 11)
     analysis_send(0)
     pl.semaphore_wait(passed, 2)
-    send(wall.at[block], wall.at[block], alike[0], 11)
     analysis_middle(0)
-    arrived(wall, 3, 11)
+    arrived(wall, 2, 11)
+    low, high = pl.ds(0, 16), pl.ds(16, 16)
+    send(wall.at[up, low], wall.at[up, low], alike[2], 12)
+    send(wall.at[down, high], wall.at[down, high], alike[1], 12)
+    arrived(wall, 1, 12)
     inside = lax.broadcasted_iota(jnp.int32, (128, 128), 0) // 32 == lax.broadcasted_iota(jnp.int32, (128, 128), 1) // 32
     for i in range(4):
         for part in range(4):
@@ -380,7 +385,8 @@
     sent(g1recv, 31, 8)
     sent(g2recv, 15, 9)
     sent(g3recv, 31, 10)
-    sent(wall, 3, 11)
+    sent(wall, 2, 11)
+    sent(wall, 1, 12)
 
 
 def publish(*refs):
@@ -421,7 +427,7 @@
         pltpu.VMEM((2, 8, 16, 128), BF), pltpu.VMEM((2, 32, 16, 128), BF),
         pltpu.VMEM((32, 2, 128), F32), pltpu.VMEM((32, 2, 128), F32),
         pltpu.VMEM((2, 128), F32), pltpu.VMEM((16, 2, 128), F32), pltpu.VMEM((32, 2, 128), F32),
-        pltpu.SemaphoreType.DMA((13,)), pltpu.SemaphoreType.DMA((12,)), pltpu.SemaphoreType.DMA((12,)), pltpu.SemaphoreType.REGULAR,
+        pltpu.SemaphoreType.DMA((13,)), pltpu.SemaphoreType.DMA((13,)), pltpu.SemaphoreType.DMA((13,)), pltpu.SemaphoreType.REGULAR,
     ]
     results = pl.pallas_call(
         kernel,

time: 63.1 us -> 62.4 us (0.989)
    pallas_call x1, Pallas kernels: 61.5 us -> 60.9 us  [body(): pl.pallas_call(kernel, out_shape=outputs, in_specs=[pl.BlockSpec(memory_s...]
where the time goes in v5:
time: 62.4 us; the launch traced here: 62.3 us
  Pallas kernels  61.7 us (99%)
  between operations  0.64 us (1%)
    pallas_call x1, Pallas kernels, body(): pl.pallas_call(kernel, out_shape=outputs, in_specs=[pl.BlockSpec(memory_s...  60.9 us

profile of v5, /device:TPU:1, one launch (start us, length us, event | category | flops | bytes accessed | tf_op | source)
XLA Modules:
  0.0 62.3 jit_solution(17069663921897000117)
XLA Ops:
  0.6 60.9 %step.1 = (f32[8,128]{1,0:T(8,128)S(1)}, bf16[256,128]{1,0:T(8,128)(2,1)S(1)}, f32[4,2,2,32,32]{4,3,2,1,0:T(8,128)S(1)}, f32[32,32]{1,0:T(8,128)S(1)}, f32[32,128]{1,0:T(8,128)S(1)}) custom-call(bf16[256,128]{1,0:T(8,128)(2,1)} %bitcast.7, f32[4,2,2,32,32]{4,3,2,1,0:T(8,128)} %w_hbm.1, bf16[32,32]{1,0:T(8,128)(2,1)} %mix_hbm.1, f32[1,32]{1,0:T(1,128)} %bitcast.9, ...), custom_call_target="tpu_custom_call" | custom-call | tf_op jit(solution)/shard_map/step/pallas_call | solution.py:432
  61.5 0.8 %publish.1 = (f32[8,128]{1,0:T(8,128)}, bf16[256,128]{1,0:T(8,128)(2,1)}, f32[4,2,2,32,32]{4,3,2,1,0:T(8,128)}, f32[32,32]{1,0:T(8,128)}, f32[32,128]{1,0:T(8,128)}) custom-call(f32[8,128]{1,0:T(8,128)S(1)} %get-tuple-element.15.refs_0_, bf16[256,128]{1,0:T(8,128)(2,1)S(1)} %get-tuple-element.16.refs_1_, f32[4,2,2,32,32]{4,3,2,1,0:T(8,128)S(1)} %get-tuple-element.17.refs_2_, ...), custom_call_target="tpu_custom_call" | custom-call | tf_op jit(solution)/shard_map/publish/pallas_call | solution.py:441
